TPU v7x, 32 devices: a whole 2x2x4 slice. The times are simulated.
32 devices in a mesh: gx: 2 (over core), gy: 4 (over y, x), gz: 4 (over z).
Axes of the slice: x: 2, y: 2, z: 4, core: 2. Of those that a mesh axis runs over, the one named last changes fastest.
Arguments:
- heights: float32 [8192, 1024], P(('gy', 'gz'), 'gx'), may hold values from -6 to 6
- scene_ids: int32 [8192, 1024], P(('gy', 'gz'), 'gx'), may hold values from 0 to 15, as said below
- scene_offset: float32 [16], replicated, may hold values from -4 to 4
- scene_weight: float32 [16], replicated, may hold values from 0.2 to 5
- band_gain: float32 [6], replicated, may hold values from 0.3 to 1.5
Outputs:
- blended: float32 [8192, 1024], P(('gy', 'gz'), 'gx')
Inputs may be any that keep to these rules, and one draw needn't show every extreme that they name: `scene_ids`: scene index of each cell.
All inputs are finite; a program needn't handle non-finite values.
Results may differ from a plain program's by a relative error of at most 0.00002.
Values sent between devices are 32-bit elements; how exact they have to be, the bound alone decides.
A program may use at most 128 MiB of HBM per device.

v0:
```python
import jax
import jax.numpy as jnp
from jax import lax
from jax.sharding import PartitionSpec as P

LOC_LEVELS = 4
GLOB_LEVELS = 2
SCENES = 16


KERN = (0.0625, 0.25, 0.375, 0.25, 0.0625)


def extended(block, sides, width):
    for axis, dim in sides:
        count = lax.axis_size(axis)
        forward = [(i, i + 1) for i in range(count - 1)]
        backward = [(target, source) for source, target in forward]
        low = lax.ppermute(
            lax.slice_in_dim(block, block.shape[dim] - width, None, axis=dim), axis, forward
        )
        high = lax.ppermute(lax.slice_in_dim(block, 0, width, axis=dim), axis, backward)
        block = jnp.concatenate([low, block, high], axis=dim)
    return block


def lookup(scene_ids, table):
    acc = jnp.zeros(scene_ids.shape, jnp.float32)
    for scene in range(SCENES):
        acc = acc + jnp.where(scene_ids == scene, table[scene], jnp.float32(0.0))
    return acc


def reduce_padded(padded):
    rows_out = padded.shape[-2] - 4
    cols_out = padded.shape[-1] - 4
    rows = KERN[0] * padded[..., 0:rows_out:2, :]
    for tap in range(1, 5):
        rows = rows + KERN[tap] * padded[..., tap : tap + rows_out : 2, :]
    result = KERN[0] * rows[..., 0:cols_out:2]
    for tap in range(1, 5):
        result = result + KERN[tap] * rows[..., tap : tap + cols_out : 2]
    return result


def expand_padded(padded):
    count = padded.shape[-2] - 2
    even = (
        padded[..., 0:count, :]
        + 6.0 * padded[..., 1 : count + 1, :]
        + padded[..., 2 : count + 2, :]
    ) * 0.125
    odd = (padded[..., 1 : count + 1, :] + padded[..., 2 : count + 2, :]) * 0.5
    rows = jnp.stack([even, odd], axis=-2)
    rows = rows.reshape(rows.shape[:-3] + (2 * count, rows.shape[-1]))
    width = rows.shape[-1] - 2
    even = (rows[..., 0:width] + 6.0 * rows[..., 1 : width + 1] + rows[..., 2 : width + 2]) * 0.125
    odd = (rows[..., 1 : width + 1] + rows[..., 2 : width + 2]) * 0.5
    result = jnp.stack([even, odd], axis=-1)
    return result.reshape(result.shape[:-2] + (2 * width,))


def pad_grid(pair, margin):
    return jnp.pad(pair, ((0, 0), (margin, margin), (margin, margin)))


def reduce_level(pair):
    rimmed = extended(pair, (("gx", 2), (("gy", "gz"), 1)), 2)
    return reduce_padded(rimmed)


def rim_up(stacked):
    return extended(stacked, (("gx", 2), (("gy", "gz"), 1)), 1)


def local(heights, scene_ids, scene_offset, scene_weight, band_gain):
    weight = lookup(scene_ids, scene_weight)
    offset = lookup(scene_ids, scene_offset)
    pair = jnp.stack([weight * (heights + offset), weight])
    ratios = [pair[0] / pair[1]]
    tile_levels = LOC_LEVELS
    for level in range(tile_levels):
        pair = reduce_level(pair)
        ratios.append(pair[0] / pair[1])
    coarse = pair.shape[1]
    size_z = lax.axis_size("gz")
    strip = lax.all_gather(pair, "gx", axis=2, tiled=True)
    strip = lax.all_gather(strip, "gz", axis=1, tiled=True)
    whole = lax.all_gather(strip, "gy", axis=1, tiled=True)
    grid_ratios = [whole[0] / whole[1]]
    for level in range(GLOB_LEVELS):
        whole = reduce_padded(pad_grid(whole, 2))
        grid_ratios.append(whole[0] / whole[1])
    top_mean = jnp.sum(whole[0]) / jnp.sum(whole[1])
    collapsed = jnp.zeros_like(grid_ratios[GLOB_LEVELS]) + top_mean
    for level in range(GLOB_LEVELS - 1, -1, -1):
        band = grid_ratios[level] - expand_padded(jnp.pad(grid_ratios[level + 1], 1))
        collapsed = band_gain[LOC_LEVELS + level] * band + expand_padded(jnp.pad(collapsed, 1))
    top = pad_grid(jnp.stack([grid_ratios[0], collapsed]), 1)
    row_block = lax.axis_index("gy") * size_z + lax.axis_index("gz")
    col_block = lax.axis_index("gx")
    piece = lax.dynamic_slice(
        top, (jnp.int32(0), row_block * coarse, col_block * coarse), (2, coarse + 2, coarse + 2)
    )
    for level in range(LOC_LEVELS - 1, -1, -1):
        expanded = expand_padded(piece)
        blended = band_gain[level] * (ratios[level] - expanded[0]) + expanded[1]
        if level > 0:
            piece = rim_up(jnp.stack([ratios[level], blended]))
    return blended


def solution(mesh):
    placed = (P(("gy", "gz"), "gx"), P(("gy", "gz"), "gx"), P(), P(), P())
    return jax.shard_map(
        local, mesh=mesh, in_specs=placed, out_specs=P(("gy", "gz"), "gx"), check_vma=False
    )
```

profile of v0, /device:TPU:4, one launch (start us, length us, event | category | flops | bytes accessed | tf_op | source)
XLA Modules:
  0.0 558.5 jit_solution(3190305298259061089)
XLA Ops:
  2.0 2.7 broadcast_compare_fusion.15
  6.2 23.3 %add_multiply_fusion = (f32[512,512]{0,1:T(8,128)S(1)}, f32[512,512]{0,1:T(8,128)S(1)}) fusion(f32[512,512]{0,1:T(8,128)S(1)} %copy.202, pred[512,512]{0,1:T(8,128)(4,1)S(1)} %get-tuple-element.31, pred[512,512]{0,1:T(8,128)(4,1)S(1)} %get-tuple-element.32, pred[512,512]{0,1:T(8,128)(4,1)S(1)} %get-tuple-element.33, ...), kind=kLoop, calls=%fused_computation.14 | loop fusion | flops 16777216 | bytes 7340160 | tf_op jit(solution)/shard_map/mul | solution.py:79
  30.8 3.0 collective-permute-start
  36.7 6.4 %collective-permute-start.3 = (f32[2,2,516]{2,1,0:T(2,128)S(1)}, f32[2,2,516]{2,1,0:T(2,128)S(1)}, u32[]{:S(2)}, u32[]{:S(2)}) collective-permute-start(f32[2,2,516]{2,1,0:T(2,128)S(1)} %copy.204), channel_id=1, source_target_pairs={{1,0},{2,1},{3,2},{4,3},{5,4},{6,5},{7,6},{8,7},{9,8},{10,9},{11,1... | collective-permute-start | bytes 24776 | tf_op jit(solution)/shard_map/ppermute | solution.py:22
  43.3 2.1 collective-permute-start.2
  45.4 39.8 %slice.657 = f32[2,256,516]{1,2,0:T(8,128)} slice(f32[2,512,516]{1,2,0:T(8,128)} %copy-done), slice={[0:2:1], [0:512:2], [0:516:1]} | slice | bytes 2113536 | tf_op jit(solution)/shard_map/slice | solution.py:39
  85.7 2.6 pad_maximum_fusion
  88.3 39.9 %slice.659 = f32[2,256,516]{1,2,0:T(8,128)} slice(f32[2,516,516]{1,2,0:T(8,128)} %pad_maximum_fusion), slice={[0:2:1], [4:516:2], [0:516:1]} | slice | bytes 2113536 | tf_op jit(solution)/shard_map/slice | solution.py:39
  128.2 39.9 %slice.658 = f32[2,256,516]{1,2,0:T(8,128)} slice(f32[2,516,516]{1,2,0:T(8,128)} %pad_maximum_fusion), slice={[0:2:1], [3:515:2], [0:516:1]} | slice | bytes 2113536 | tf_op jit(solution)/shard_map/slice | solution.py:39
  168.0 40.0 %slice.656 = f32[2,256,516]{1,2,0:T(8,128)} slice(f32[2,516,516]{1,2,0:T(8,128)} %pad_maximum_fusion), slice={[0:2:1], [1:513:2], [0:516:1]} | slice | bytes 2113536 | tf_op jit(solution)/shard_map/slice | solution.py:39
  208.1 39.8 %slice.655 = f32[2,256,516]{1,2,0:T(8,128)} slice(f32[2,516,516]{1,2,0:T(8,128)} %pad_maximum_fusion), slice={[0:2:1], [0:512:2], [0:516:1]} | slice | bytes 2113536 | tf_op jit(solution)/shard_map/slice | solution.py:37
  247.9 2.9 multiply_add_fusion
  250.8 2.2 slice.664
  253.0 2.2 slice.663
  255.2 2.2 slice.662
  257.4 2.1 slice.661
  259.5 2.2 slice.660
  261.7 1.8 multiply_add_fusion.2
  264.8 3.0 collective-permute-start.4
  269.6 7.5 %collective-permute-start.7 = (f32[2,2,260]{1,2,0:T(8,128)}, f32[2,2,260]{1,2,0:T(8,128)S(1)}, u32[]{:S(2)}, u32[]{:S(2)}) collective-permute-start(f32[2,2,260]{1,2,0:T(8,128)} %get-tuple-element.49), channel_id=1, source_target_pairs={{1,0},{2,1},{3,2},{4,3},{5,4},{6,5},{7,6},{8,7},{9,8},{10,9},{11,1... | collective-permute-start | bytes 12488 | tf_op jit(solution)/shard_map/ppermute | solution.py:22
  277.1 1.9 collective-permute-start.6
  279.0 10.4 %slice.674 = f32[2,128,260]{1,2,0:T(8,128)} slice(f32[2,256,260]{1,2,0:T(8,128)S(1)} %pad_maximum_fusion.13), slice={[0:2:1], [0:256:2], [0:260:1]} | slice | bytes 532480 | tf_op jit(solution)/shard_map/slice | solution.py:39
  292.8 10.1 %slice.676 = f32[2,128,260]{1,2,0:T(8,128)} slice(f32[2,260,260]{1,2,0:T(8,128)S(1)} %pad_maximum_fusion.4), slice={[0:2:1], [4:260:2], [0:260:1]} | slice | bytes 532480 | tf_op jit(solution)/shard_map/slice | solution.py:39
  302.8 10.0 %slice.675 = f32[2,128,260]{1,2,0:T(8,128)} slice(f32[2,260,260]{1,2,0:T(8,128)S(1)} %pad_maximum_fusion.4), slice={[0:2:1], [3:259:2], [0:260:1]} | slice | bytes 532480 | tf_op jit(solution)/shard_map/slice | solution.py:39
  312.8 10.1 %slice.673 = f32[2,128,260]{1,2,0:T(8,128)} slice(f32[2,260,260]{1,2,0:T(8,128)S(1)} %pad_maximum_fusion.4), slice={[0:2:1], [1:257:2], [0:260:1]} | slice | bytes 532480 | tf_op jit(solution)/shard_map/slice | solution.py:39
  323.0 10.0 %slice.672 = f32[2,128,260]{1,2,0:T(8,128)} slice(f32[2,260,260]{1,2,0:T(8,128)S(1)} %pad_maximum_fusion.4), slice={[0:2:1], [0:256:2], [0:260:1]} | slice | bytes 532480 | tf_op jit(solution)/shard_map/slice | solution.py:37
  338.1 3.0 collective-permute-start.8
  342.7 6.3 %collective-permute-start.11 = (f32[2,2,132]{1,2,0:T(8,128)}, f32[2,2,132]{1,2,0:T(8,128)S(1)}, u32[]{:S(2)}, u32[]{:S(2)}) collective-permute-start(f32[2,2,132]{1,2,0:T(8,128)} %get-tuple-element.72), channel_id=1, source_target_pairs={{1,0},{2,1},{3,2},{4,3},{5,4},{6,5},{7,6},{8,7},{9,8},{10,9},{11,1... | collective-permute-start | bytes 6344 | tf_op jit(solution)/shard_map/ppermute | solution.py:22
  349.0 2.1 collective-permute-start.10
  351.1 2.3 slice.691
  353.4 6.7 %collective-permute-done.10 = f32[2,2,132]{1,2,0:T(8,128)S(1)} collective-permute-done((f32[2,2,132]{1,2,0:T(8,128)S(1)}, f32[2,2,132]{1,2,0:T(8,128)S(1)}, u32[]{:S(2)}, u32[]{:S(2)}) %collective-permute-start.10) | collective-permute-done | bytes 2144 | tf_op jit(solution)/shard_map/ppermute | solution.py:19
  360.3 2.3 slice.693
  362.6 2.3 slice.692
  364.9 3.0 slice.690
  367.9 2.9 slice.689
  373.3 3.0 collective-permute-start.12
  377.2 1.9 collective-permute-start.15
  379.2 3.9 collective-permute-start.14
  385.2 3.9 collective-permute-done.14
  392.1 1.9 all_gather.9
  394.0 13.4 %all_gather.10 = f32[2,128,64]{2,0,1:T(2,128)S(1)} all-gather(f32[2,32,64]{2,0,1:T(2,128)S(1)} %copy.207), channel_id=1, replica_groups=mesh['gx'=2,'gy'=4,'gz'=4] {'gz'}, dimensions={1}, use_global_device_ids=true | all-gather | bytes 81920 | tf_op jit(solution)/shard_map/all_gather | solution.py:88
  407.5 8.6 %all_gather.11 = f32[2,512,64]{1,2,0:T(8,128)S(1)} all-gather(f32[2,128,64]{1,2,0:T(8,128)S(1)} %copy.208), channel_id=1, replica_groups=mesh['gx'=2,'gy'=4,'gz'=4] {'gy'}, dimensions={1}, use_global_device_ids=true | all-gather | bytes 327680 | tf_op jit(solution)/shard_map/all_gather | solution.py:89
  416.2 5.3 slice.723
  421.5 5.3 slice.722
  426.8 5.3 slice.721
  432.1 5.5 slice.720
  437.6 5.3 slice.719
  477.1 3.0 collective-permute-start.16
  481.0 3.2 collective-permute-start.19
  484.3 2.6 collective-permute-start.18
  487.6 6.5 %collective-permute-done.18 = f32[2,1,66]{1,2,0:T(8,128)S(1)} collective-permute-done((f32[2,1,66]{1,2,0:T(8,128)S(1)}, f32[2,1,66]{1,2,0:T(8,128)S(1)}, u32[]{:S(2)}, u32[]{:S(2)}) %collective-permute-start.18) | collective-permute-done | bytes 560 | tf_op jit(solution)/shard_map/ppermute | solution.py:19
  496.7 3.0 collective-permute-start.20
  500.6 1.9 collective-permute-start.23
  502.6 3.9 collective-permute-start.22
  506.5 2.0 collective-permute-done.23
  508.6 5.4 collective-permute-done.22
  517.7 3.0 collective-permute-start.24
  521.7 1.9 collective-permute-start.27
  523.6 3.9 collective-permute-start.26
  527.5 10.6 %collective-permute-done.27 = f32[2,1,258]{1,2,0:T(8,128)S(1)} collective-permute-done((f32[2,1,258]{1,2,0:T(8,128)S(1)}, f32[2,1,258]{1,2,0:T(8,128)S(1)}, u32[]{:S(2)}, u32[]{:S(2)}) %collective-permute-start.27) | collective-permute-done | bytes 2096 | tf_op jit(solution)/shard_map/ppermute | solution.py:22
  538.9 2.2 copy.247
  541.1 4.9 fusion.67
  549.4 1.7 squeeze.197
  554.4 2.6 multiply_add_fusion.1
  (207 shorter events, 81.0 us)
Async XLA Ops:
  0.0 1.7 copy-start.1
  2.0 2.7 copy-start.3
  2.0 3.5 copy-start.4
  29.5 4.3 collective-permute-start.1
  30.8 3.8 collective-permute-start
  34.9 1.3 copy-start
  36.7 48.5 %collective-permute-start.3 = (f32[2,2,516]{2,1,0:T(2,128)S(1)}, f32[2,2,516]{2,1,0:T(2,128)S(1)}, u32[]{:S(2)}, u32[]{:S(2)}) collective-permute-start(f32[2,2,516]{2,1,0:T(2,128)S(1)} %copy.204), channel_id=1, source_target_pairs={{1,0},{2,1},{3,2},{4,3},{5,4},{6,5},{7,6},{8,7},{9,8},{10,9},{11,1... | collective-permute-start | bytes 24776 | tf_op jit(solution)/shard_map/ppermute | solution.py:22
  43.3 42.2 %collective-permute-start.2 = (f32[2,2,516]{2,1,0:T(2,128)S(1)}, f32[2,2,516]{2,1,0:T(2,128)S(1)}, u32[]{:S(2)}, u32[]{:S(2)}) collective-permute-start(f32[2,2,516]{2,1,0:T(2,128)S(1)} %copy.203), channel_id=1, source_target_pairs={{0,1},{1,2},{2,3},{3,4},{4,5},{5,6},{6,7},{7,8},{8,9},{9,10},{10,1... | collective-permute-start | bytes 24776 | tf_op jit(solution)/shard_map/ppermute | solution.py:19
  263.5 4.3 collective-permute-start.5
  264.8 3.8 collective-permute-start.4
  269.6 19.8 %collective-permute-start.7 = (f32[2,2,260]{1,2,0:T(8,128)}, f32[2,2,260]{1,2,0:T(8,128)S(1)}, u32[]{:S(2)}, u32[]{:S(2)}) collective-permute-start(f32[2,2,260]{1,2,0:T(8,128)} %get-tuple-element.49), channel_id=1, source_target_pairs={{1,0},{2,1},{3,2},{4,3},{5,4},{6,5},{7,6},{8,7},{9,8},{10,9},{11,1... | collective-permute-start | bytes 12488 | tf_op jit(solution)/shard_map/ppermute | solution.py:22
  277.1 14.3 %collective-permute-start.6 = (f32[2,2,260]{1,2,0:T(8,128)}, f32[2,2,260]{1,2,0:T(8,128)}, u32[]{:S(2)}, u32[]{:S(2)}) collective-permute-start(f32[2,2,260]{1,2,0:T(8,128)} %get-tuple-element.48), channel_id=1, source_target_pairs={{0,1},{1,2},{2,3},{3,4},{4,5},{5,6},{6,7},{7,8},{8,9},{9,10},{10,1... | collective-permute-start | bytes 12488 | tf_op jit(solution)/shard_map/ppermute | solution.py:19
  289.4 0.7 copy-start.2
  336.8 4.3 collective-permute-start.9
  338.1 3.8 collective-permute-start.8
  342.7 10.7 %collective-permute-start.11 = (f32[2,2,132]{1,2,0:T(8,128)}, f32[2,2,132]{1,2,0:T(8,128)S(1)}, u32[]{:S(2)}, u32[]{:S(2)}) collective-permute-start(f32[2,2,132]{1,2,0:T(8,128)} %get-tuple-element.72), channel_id=1, source_target_pairs={{1,0},{2,1},{3,2},{4,3},{5,4},{6,5},{7,6},{8,7},{9,8},{10,9},{11,1... | collective-permute-start | bytes 6344 | tf_op jit(solution)/shard_map/ppermute | solution.py:22
  349.0 11.1 %collective-permute-start.10 = (f32[2,2,132]{1,2,0:T(8,128)S(1)}, f32[2,2,132]{1,2,0:T(8,128)S(1)}, u32[]{:S(2)}, u32[]{:S(2)}) collective-permute-start(f32[2,2,132]{1,2,0:T(8,128)S(1)} %get-tuple-element.71), channel_id=1, source_target_pairs={{0,1},{1,2},{2,3},{3,4},{4,5},{5,6},{6,7},{7,8},{8,9},{9,10},{10,1... | collective-permute-start | bytes 6344 | tf_op jit(solution)/shard_map/ppermute | solution.py:19
  367.9 8.5 %copy-start.5 = (f32[6]{0:T(128)S(1)}, f32[6]{0:T(128)}, u32[]{:S(2)}) copy-start(f32[6]{0:T(128)} %param.9) | copy-start | bytes 76
  372.0 5.0 collective-permute-start.13
  373.3 3.8 collective-permute-start.12
  377.2 8.0 %collective-permute-start.15 = (f32[2,2,68]{1,2,0:T(8,128)S(1)}, f32[2,2,68]{1,2,0:T(8,128)S(1)}, u32[]{:S(2)}, u32[]{:S(2)}) collective-permute-start(f32[2,2,68]{1,2,0:T(8,128)S(1)} %get-tuple-element.94), channel_id=1, source_target_pairs={{1,0},{2,1},{3,2},{4,3},{5,4},{6,5},{7,6},{8,7},{9,8},{10,9},{11,1... | collective-permute-start | bytes 3272 | tf_op jit(solution)/shard_map/ppermute | solution.py:22
  379.2 10.0 %collective-permute-start.14 = (f32[2,2,68]{1,2,0:T(8,128)S(1)}, f32[2,2,68]{1,2,0:T(8,128)S(1)}, u32[]{:S(2)}, u32[]{:S(2)}) collective-permute-start(f32[2,2,68]{1,2,0:T(8,128)S(1)} %get-tuple-element.93), channel_id=1, source_target_pairs={{0,1},{1,2},{2,3},{3,4},{4,5},{5,6},{6,7},{7,8},{8,9},{9,10},{10,1... | collective-permute-start | bytes 3272 | tf_op jit(solution)/shard_map/ppermute | solution.py:19
  475.8 4.3 collective-permute-start.17
  477.1 3.8 collective-permute-start.16
  481.0 6.4 %collective-permute-start.19 = (f32[2,1,66]{1,2,0:T(8,128)S(1)}, f32[2,1,66]{1,2,0:T(8,128)S(1)}, u32[]{:S(2)}, u32[]{:S(2)}) collective-permute-start(f32[2,1,66]{1,2,0:T(8,128)S(1)} %get-tuple-element.92), channel_id=1, source_target_pairs={{1,0},{2,1},{3,2},{4,3},{5,4},{6,5},{7,6},{8,7},{9,8},{10,9},{11,1... | collective-permute-start | bytes 1592 | tf_op jit(solution)/shard_map/ppermute | solution.py:22
  484.3 9.8 %collective-permute-start.18 = (f32[2,1,66]{1,2,0:T(8,128)S(1)}, f32[2,1,66]{1,2,0:T(8,128)S(1)}, u32[]{:S(2)}, u32[]{:S(2)}) collective-permute-start(f32[2,1,66]{1,2,0:T(8,128)S(1)} %get-tuple-element.91), channel_id=1, source_target_pairs={{0,1},{1,2},{2,3},{3,4},{4,5},{5,6},{6,7},{7,8},{8,9},{9,10},{10,1... | collective-permute-start | bytes 1592 | tf_op jit(solution)/shard_map/ppermute | solution.py:19
  495.4 4.3 collective-permute-start.21
  496.7 3.8 collective-permute-start.20
  500.6 7.8 %collective-permute-start.23 = (f32[2,1,130]{1,2,0:T(8,128)S(1)}, f32[2,1,130]{1,2,0:T(8,128)S(1)}, u32[]{:S(2)}, u32[]{:S(2)}) collective-permute-start(f32[2,1,130]{1,2,0:T(8,128)S(1)} %get-tuple-element.70), channel_id=1, source_target_pairs={{1,0},{2,1},{3,2},{4,3},{5,4},{6,5},{7,6},{8,7},{9,8},{10,9},{11,1... | collective-permute-start | bytes 3128 | tf_op jit(solution)/shard_map/ppermute | solution.py:22
  502.6 11.4 %collective-permute-start.22 = (f32[2,1,130]{1,2,0:T(8,128)S(1)}, f32[2,1,130]{1,2,0:T(8,128)S(1)}, u32[]{:S(2)}, u32[]{:S(2)}) collective-permute-start(f32[2,1,130]{1,2,0:T(8,128)S(1)} %get-tuple-element.69), channel_id=1, source_target_pairs={{0,1},{1,2},{2,3},{3,4},{4,5},{5,6},{6,7},{7,8},{8,9},{9,10},{10,1... | collective-permute-start | bytes 3128 | tf_op jit(solution)/shard_map/ppermute | solution.py:19
  516.4 4.3 collective-permute-start.25
  517.7 3.8 collective-permute-start.24
  521.7 16.4 %collective-permute-start.27 = (f32[2,1,258]{1,2,0:T(8,128)S(1)}, f32[2,1,258]{1,2,0:T(8,128)S(1)}, u32[]{:S(2)}, u32[]{:S(2)}) collective-permute-start(f32[2,1,258]{1,2,0:T(8,128)S(1)} %get-tuple-element.47), channel_id=1, source_target_pairs={{1,0},{2,1},{3,2},{4,3},{5,4},{6,5},{7,6},{8,7},{9,8},{10,9},{11,1... | collective-permute-start | bytes 6200 | tf_op jit(solution)/shard_map/ppermute | solution.py:22
  523.6 14.8 %collective-permute-start.26 = (f32[2,1,258]{1,2,0:T(8,128)S(1)}, f32[2,1,258]{1,2,0:T(8,128)S(1)}, u32[]{:S(2)}, u32[]{:S(2)}) collective-permute-start(f32[2,1,258]{1,2,0:T(8,128)S(1)} %get-tuple-element.46), channel_id=1, source_target_pairs={{0,1},{1,2},{2,3},{3,4},{4,5},{5,6},{6,7},{7,8},{8,9},{9,10},{10,1... | collective-permute-start | bytes 6200 | tf_op jit(solution)/shard_map/ppermute | solution.py:19
where the time goes:
time: 564 us; the launch traced here: 559 us
  local copies, waits for them, and re-layouts  356 us (63%)
  starting transfers between devices  79.9 us (14%)
  other arithmetic  53.1 us (9%)
  waiting for transfers between devices  43.2 us (8%)
  blocking collectives  23.8 us (4%)
    slice x24, local copies, waits for them, and re-layouts, reduce_padded(): rows = rows + KERN[tap] * padded[..., tap:tap + rows_out:2, :]  239 us
    slice x6, local copies, waits for them, and re-layouts, reduce_padded(): rows = KERN[0] * padded[..., 0:rows_out:2, :]  59.9 us
    ppermute x14, starting transfers between devices, extended(): lax.ppermute(lax.slice_in_dim(block, block.shape[dim] - width, None, axis...  41.7 us
    ppermute x14, starting transfers between devices, extended(): lax.ppermute(lax.slice_in_dim(block, 0, width, axis=dim), axis, backward)  38.2 us
    ppermute x14, waiting for transfers between devices, extended(): lax.ppermute(lax.slice_in_dim(block, block.shape[dim] - width, None, axis...  28.6 us
    mul x1, other arithmetic, local(): pair = jnp.stack([weight * (heights + offset), weight])  23.3 us
    ppermute x14, waiting for transfers between devices, extended(): lax.ppermute(lax.slice_in_dim(block, 0, width, axis=dim), axis, backward)  14.6 us
    unnamed x26, local copies, waits for them, and re-layouts  14.4 us
  transfers between devices with their start and end apart: 28, of which 16 were waited for; matrix products, arithmetic and copies ran while one was open for 10% of the time, Pallas kernels for 0%

commit v1 on v0

v1 whole, which is shorter than its diff:
```python
import functools

import jax
import jax.numpy as jnp
import numpy as np
from jax import lax
from jax.experimental import pallas as pl
from jax.experimental.pallas import tpu as pltpu
from jax.sharding import PartitionSpec as P

F32, BF16 = jnp.float32, jnp.bfloat16
FAR = 1 << 20
HALO = 16
SIDE = 128
EDGE3 = 24
TAPS = (0.375, 0.25, 0.0625)
LEVELS = 6


def reach(count):
    weights = np.ones(count >> LEVELS, np.float64)
    for _ in range(LEVELS):
        fine = np.zeros(2 * weights.size + 4, np.float64)
        for tap, value in zip(range(-2, 3), (0.0625, 0.25, 0.375, 0.25, 0.0625)):
            fine[2 + tap : 2 + tap + 2 * weights.size : 2] += value * weights
        weights = fine[2:-2]
    return weights.astype(np.float32)


def split(x):
    high = x.astype(BF16)
    return high, (x - high.astype(F32)).astype(BF16)


def right(x, c):
    high, low = split(x)
    return jnp.dot(high, c, preferred_element_type=F32) + jnp.dot(
        low, c, preferred_element_type=F32
    )


def left(r, x):
    high, low = split(x)
    return jnp.dot(r, high, preferred_element_type=F32) + jnp.dot(
        r, low, preferred_element_type=F32
    )


def band(distance, scale):
    far = jnp.abs(distance)
    value = jnp.where(far == 2, TAPS[2] * scale, 0.0)
    value = jnp.where(far == 1, TAPS[1] * scale, value)
    value = jnp.where(far == 0, TAPS[0] * scale, value)
    return value.astype(F32).astype(BF16)


def kernel(
    sizes, off_ref, wgt_ref, gain_ref, h_ref, s_ref, u_ref, v_ref, out_ref,
    h_buf, s_buf, u_buf, v_buf, nh, nl, dh, dl, b3, part, slots,
    own_sem, send0, recv0, send3, recv3, psend, precv,
):
    nr, nc, nx, ny, nz, rows_total, cols_total = sizes
    cx, cy, cz = lax.axis_index("gx"), lax.axis_index("gy"), lax.axis_index("gz")
    row = cy * nz + cz
    blocks = ny * nz
    w3 = nc // 8
    t3 = nr // 8

    def device(drow, dcol):
        target = row + drow
        return {"gx": cx + dcol, "gy": target // nz, "gz": target % nz}

    has = {-1: (row > 0, cx > 0), 0: None, 1: (row < blocks - 1, cx < nx - 1)}

    def there(drow, dcol):
        ok = None
        if drow:
            ok = has[drow][0]
        if dcol:
            ok = has[dcol][1] if ok is None else jnp.logical_and(ok, has[dcol][1])
        return ok

    dirs = [(a, b) for a in (-1, 0, 1) for b in (-1, 0, 1) if a or b]
    axes = (("gx", nx, cx), ("gz", nz, cz), ("gy", ny, cy))

    own = []
    for i, (src, dst) in enumerate(
        (
            (h_ref, h_buf.at[pl.ds(0, nr), pl.ds(0, nc)]),
            (s_ref, s_buf.at[pl.ds(0, nr), pl.ds(0, nc)]),
            (u_ref.at[row], u_buf),
            (v_ref.at[cx], v_buf),
        )
    ):
        copy = pltpu.make_async_copy(src, dst, own_sem.at[i])
        copy.start()
        own.append(copy)

    barrier = pltpu.get_barrier_semaphore()
    for d in dirs:
        @pl.when(there(*d))
        def _():
            pl.semaphore_signal(barrier, inc=1, device_id=device(*d))
    for name, count, me in axes:
        for step in range(1, count):
            pl.semaphore_signal(barrier, inc=1, device_id={name: (me + step) % count})

    def iota(n, dim):
        return lax.broadcasted_iota(jnp.int32, (n, 1) if dim == 0 else (1, n), dim)

    def fold(index, first, total, level):
        base = first >> level
        ok = jnp.logical_and(index + base >= 0, index + base < (total >> level))
        return jnp.where(ok, index, FAR)

    row0, col0 = row * nr, cx * nc
    r1, r2 = nr // 2 + 16, nr // 4 + 16
    c1, c2 = nc // 2 + 128, nc // 4 + 128
    r3, r4, r5, r6 = t3 + 2 * EDGE3, nr // 16 + 32, nr // 32 + 16, nr // 64 + 8

    def rows_at(level, dim):
        if level == 0:
            p = iota(nr + 2 * HALO, dim)
            return jnp.where(p < nr, p, jnp.where(p < nr + HALO, p - nr - HALO, p - HALO))
        count, shift = ((r1, 8), (r2, 8), (r3, EDGE3), (r4, 16), (r5, 8), (r6, 4))[level - 1]
        return iota(count, dim) - shift

    def cols_at(level, dim):
        if level == 0:
            p = iota(nc + 2 * SIDE, dim)
            return jnp.where(p < nc, p, jnp.where(p < nc + SIDE, p - nc - SIDE, p - SIDE))
        if level < 3:
            return iota((c1, c2)[level - 1], dim) - 8
        if level == 3:
            p = iota(6 * w3, dim)
            return (p // (2 * w3) - 1) * w3 + p % w3
        return iota(2 * w3, dim) % w3 - (16, 8, 4)[level - 4]

    def kind(count, dim):
        return (iota(count, dim) // w3) % 2

    def reduce_rows(level):
        out = fold(rows_at(level + 1, 0), row0, rows_total, level + 1)
        return band(rows_at(level, 1) - 2 * out, 1.0)

    def reduce_cols(level):
        out = fold(cols_at(level + 1, 1), col0, cols_total, level + 1)
        distance = cols_at(level, 0) - 2 * out
        if level >= 3:
            same = kind(distance.shape[0], 0) == kind(distance.shape[1], 1)
            distance = jnp.where(same, distance, FAR)
        return band(distance, 1.0)

    def expand_rows(level):
        out = iota(nr, 0) if level == 0 else rows_at(level, 0)
        return band(2 * rows_at(level + 1, 1) - out, 2.0)

    def expand_cols(level):
        out = iota(nc, 1) if level == 0 else cols_at(level, 1)
        return band(2 * cols_at(level + 1, 0) - out, 2.0)

    near = sum(there(*d).astype(jnp.int32) for d in dirs)
    pl.semaphore_wait(barrier, near + (nx + ny + nz - 3))

    def rim(i, a, d):
        drow, dcol = d
        src, dst = ((h_ref, h_buf), (s_ref, s_buf))[a]
        rs = {-1: (0, nr + HALO, HALO), 0: (0, 0, nr), 1: (nr - HALO, nr, HALO)}[drow]
        cs = {-1: (0, nc + SIDE, SIDE), 0: (0, 0, nc), 1: (nc - SIDE, nc, SIDE)}[dcol]
        return pltpu.make_async_remote_copy(
            src_ref=src.at[pl.ds(rs[0], rs[2]), pl.ds(cs[0], cs[2])],
            dst_ref=dst.at[pl.ds(rs[1], rs[2]), pl.ds(cs[1], cs[2])],
            send_sem=send0.at[2 * i + a],
            recv_sem=recv0.at[2 * i + a],
            device_id=device(*d),
        )

    for i, d in enumerate(dirs):
        @pl.when(there(*d))
        def _():
            for a in range(2):
                rim(i, a, d).start()

    def lookup(masks, table):
        values = [table[i] for i in range(table.shape[0])]
        for mask in masks:
            values = [
                jnp.where(mask, values[i + 1], values[i]) for i in range(0, len(values), 2)
            ]
        return values[0]

    bits = (off_ref.shape[0] - 1).bit_length()

    def level0(rows, cols, valid):
        ids = s_buf[rows, cols]
        masks = [(ids & (1 << bit)) != 0 for bit in range(bits)]
        weight = lookup(masks, wgt_ref)
        moved = h_buf[rows, cols] + lookup(masks, off_ref)
        numer = weight * moved
        if valid is not None:
            weight = jnp.where(valid, weight, 0.0)
            numer = jnp.where(valid, numer, 0.0)
        nh[rows, cols], nl[rows, cols] = split(numer)
        dh[rows, cols], dl[rows, cols] = split(weight)
        return moved

    for copy in own:
        copy.wait()

    step = 32

    def own_rows(i, carry):
        rows = pl.ds(pl.multiple_of(i * step, step), step)
        out_ref[rows, :] = level0(rows, pl.ds(0, nc), None)
        return carry

    lax.fori_loop(0, nr // step, own_rows, 0)

    reduce0 = reduce_rows(0)
    u_high, u_low = split(u_buf[...])
    pick = iota(16, 0)
    u_rows = jnp.where(
        pick == 0, u_high.astype(F32), jnp.where(pick == 1, u_low.astype(F32), 0.0)
    ).astype(BF16)
    top = jnp.concatenate([reduce0[:, :nr], u_rows], axis=0)
    rim0 = reduce0[:, nr:]

    def dot(a, b):
        return jnp.dot(a, b, preferred_element_type=F32)

    tn = dot(top, nh[pl.ds(0, nr), pl.ds(0, nc)]) + dot(top, nl[pl.ds(0, nr), pl.ds(0, nc)])
    td = dot(top, dh[pl.ds(0, nr), pl.ds(0, nc)]) + dot(top, dl[pl.ds(0, nr), pl.ds(0, nc)])
    v_row = v_buf[...]
    sum_n = jnp.sum(tn[r1:, :] * v_row)
    sum_d = jnp.sum(td[r1:, :] * v_row)

    tile_row = lax.broadcasted_iota(jnp.int32, (8, 128), 0)
    part[0] = jnp.where(tile_row == 0, sum_n, jnp.where(tile_row == 1, sum_d, 0.0))

    starts = (0, nx - 1, nx + nz - 2)

    def phase(k):
        name, count, me = axes[k]
        return [
            pltpu.make_async_remote_copy(
                src_ref=part.at[k],
                dst_ref=slots.at[starts[k] + s - 1],
                send_sem=psend.at[starts[k] + s - 1],
                recv_sem=precv.at[starts[k] + s - 1],
                device_id={name: (me + s) % count},
            )
            for s in range(1, count)
        ]

    def finish(k):
        total = part[k]
        for s, copy in enumerate(phase(k)):
            copy.wait()
            total = total + slots[starts[k] + s]
        return total

    for copy in phase(0):
        copy.start()

    for i, d in enumerate(dirs):
        @pl.when(there(*d))
        def _():
            for a in range(2):
                rim(i, a, d).wait_send()

        @pl.when(there(-d[0], -d[1]))
        def _():
            for a in range(2):
                rim(i, a, d).wait_recv()

    def yes(flag):
        return flag.astype(jnp.int32)

    up, down = yes(row > 0), yes(row < blocks - 1)
    west, east = yes(cx > 0), yes(cx < nx - 1)

    def row_ok(p):
        return jnp.where(p < nr, 1, jnp.where(p < nr + HALO, up, down))

    level0(pl.ds(nr, 2 * HALO), pl.ds(0, nc), jnp.broadcast_to(row_ok(iota(2 * HALO, 0) + nr), (2 * HALO, nc)) > 0)
    side_ok = jnp.where(iota(2 * SIDE, 1) < SIDE, west, east)

    def side_rows(i, carry):
        rows = pl.ds(pl.multiple_of(i * step, step), step)
        level0(rows, pl.ds(nc, 2 * SIDE), (row_ok(iota(step, 0) + i * step) * side_ok) > 0)
        return carry

    lax.fori_loop(0, (nr + 2 * HALO) // step, side_rows, 0)

    rim_r, side_c = pl.ds(nr, 2 * HALO), pl.ds(nc, 2 * SIDE)
    cols0 = reduce_cols(0)

    def level1(t_own, high, low):
        t_own = t_own[:r1, :] + dot(rim0, high[rim_r, pl.ds(0, nc)]) + dot(rim0, low[rim_r, pl.ds(0, nc)])
        t_side = dot(reduce0, high[:, side_c]) + dot(reduce0, low[:, side_c])
        return right(t_own, cols0[:nc]) + right(t_side, cols0[nc:])

    n1, d1 = level1(tn, nh, nl), level1(td, dh, dl)

    part[1] = finish(0)
    for copy in phase(1):
        copy.start()

    rows1, cols1 = reduce_rows(1), reduce_cols(1)
    n2, d2 = left(rows1, right(n1, cols1)), left(rows1, right(d1, cols1))

    own_out = iota(2 * w3, 1)
    in2 = cols_at(2, 0)
    pick_n = band(jnp.where(own_out < w3, in2 - 2 * own_out, FAR), 1.0)
    pick_d = band(jnp.where(own_out < w3, FAR, in2 - 2 * (own_out - w3)), 1.0)
    own_rows3 = band(rows_at(2, 1) - 2 * iota(t3, 0), 1.0)
    both = right(n2, pick_n) + right(d2, pick_d)
    b3[1, pl.ds(EDGE3, t3), :] = left(own_rows3, both)

    def rim3(i, d):
        drow, dcol = d
        rs = {
            -1: (EDGE3, EDGE3 + t3, EDGE3),
            0: (EDGE3, EDGE3, t3),
            1: (t3, 0, EDGE3),
        }[drow]
        return pltpu.make_async_remote_copy(
            src_ref=b3.at[1, pl.ds(rs[0], rs[2]), :],
            dst_ref=b3.at[1 - dcol, pl.ds(rs[1], rs[2]), :],
            send_sem=send3.at[i],
            recv_sem=recv3.at[i],
            device_id=device(*d),
        )

    for i, d in enumerate(dirs):
        @pl.when(there(*d))
        def _():
            rim3(i, d).start()

    q1 = jnp.where(d1 > 0, n1 / d1, 0.0)
    q2 = jnp.where(d2 > 0, n2 / d2, 0.0)
    part[2] = finish(1)
    for copy in phase(2):
        copy.start()

    rows_ = [None, None, None] + [reduce_rows(level) for level in (3, 4, 5)]
    cols_ = [None, None, None] + [reduce_cols(level) for level in (3, 4, 5)]
    up_rows = [expand_rows(level) for level in range(6)]
    up_cols = [expand_cols(level) for level in range(6)]

    for i, d in enumerate(dirs):
        @pl.when(there(*d))
        def _():
            rim3(i, d).wait_send()

        @pl.when(there(-d[0], -d[1]))
        def _():
            rim3(i, d).wait_recv()

    p3 = iota(r3, 0)
    ok3 = jnp.where(p3 < EDGE3, up, jnp.where(p3 < EDGE3 + t3, 1, down))
    lane = iota(2 * w3, 1)

    def ratio(packed):
        weights = pltpu.roll(packed, w3, axis=1)
        ok = jnp.logical_and(weights > 0, jnp.broadcast_to(lane, packed.shape) < w3)
        return jnp.where(ok, packed / weights, 0.0), ok

    pieces = []
    for block, flag in ((0, west), (1, None), (2, east)):
        ok = ok3 if flag is None else ok3 * flag
        piece = b3[block]
        pieces.append(jnp.where(jnp.broadcast_to(ok, piece.shape) > 0, piece, 0.0))
    packed = jnp.concatenate(pieces, axis=1)
    q3 = [ratio(piece) for piece in pieces]
    q3, ok_3 = [q for q, _ in q3], [jnp.where(ok, 1.0, 0.0) for _, ok in q3]
    q3, ok_3 = jnp.concatenate(q3, axis=1), jnp.concatenate(ok_3, axis=1) > 0

    v4 = left(rows_[3], right(packed, cols_[3]))
    v5 = left(rows_[4], right(v4, cols_[4]))
    v6 = left(rows_[5], right(v5, cols_[5]))
    q4, ok_4 = ratio(v4)
    q5, ok_5 = ratio(v5)
    q6, ok_6 = ratio(v6)

    total = finish(2)
    top_sum = jnp.sum(jnp.where(tile_row == 0, total, 0.0), axis=0, keepdims=True)
    top_weight = jnp.sum(jnp.where(tile_row == 1, total, 0.0), axis=0, keepdims=True)
    top_mean = (top_sum / top_weight)[:, :1]

    z = jnp.where(ok_6, top_mean - gain_ref[5] * q6, 0.0)
    levels = ((5, q5, ok_5), (4, q4, ok_4), (3, q3, ok_3), (2, q2, d2 > 0), (1, q1, d1 > 0))
    for level, q, ok in levels:
        grown = left(up_rows[level], right(z, up_cols[level]))
        z = jnp.where(ok, grown + (gain_ref[level] - gain_ref[level - 1]) * q, 0.0)
    wide = right(z, up_cols[0])
    out_ref[...] = gain_ref[0] * out_ref[...] + left(up_rows[0], wide)


def local(mesh_shape, heights, scene_ids, scene_offset, scene_weight, band_gain):
    nx, ny, nz = mesh_shape
    nr, nc = heights.shape
    rows_total, cols_total = nr * ny * nz, nc * nx
    u = jnp.asarray(reach(rows_total).reshape(ny * nz, 1, nr))
    v = jnp.asarray(reach(cols_total).reshape(nx, 1, nc))
    sizes = (nr, nc, nx, ny, nz, rows_total, cols_total)
    ext = (nr + 2 * HALO, nc + 2 * SIDE)
    peers = nx + ny + nz - 3
    smem = pl.BlockSpec(memory_space=pltpu.SMEM)
    hbm = pl.BlockSpec(memory_space=pl.ANY)
    return pl.pallas_call(
        functools.partial(kernel, sizes),
        out_shape=jax.ShapeDtypeStruct((nr, nc), F32),
        in_specs=[smem, smem, smem, hbm, hbm, hbm, hbm],
        out_specs=pl.BlockSpec(memory_space=pltpu.VMEM),
        scratch_shapes=[
            pltpu.VMEM(ext, F32),
            pltpu.VMEM(ext, jnp.int32),
            pltpu.VMEM((1, nr), F32),
            pltpu.VMEM((1, nc), F32),
            pltpu.VMEM(ext, BF16),
            pltpu.VMEM(ext, BF16),
            pltpu.VMEM(ext, BF16),
            pltpu.VMEM(ext, BF16),
            pltpu.VMEM((3, nr // 8 + 2 * EDGE3, nc // 4), F32),
            pltpu.VMEM((3, 8, 128), F32),
            pltpu.VMEM((peers, 8, 128), F32),
            pltpu.SemaphoreType.DMA((4,)),
            pltpu.SemaphoreType.DMA((16,)),
            pltpu.SemaphoreType.DMA((16,)),
            pltpu.SemaphoreType.DMA((8,)),
            pltpu.SemaphoreType.DMA((8,)),
            pltpu.SemaphoreType.DMA((peers,)),
            pltpu.SemaphoreType.DMA((peers,)),
        ],
        compiler_params=pltpu.CompilerParams(collective_id=0, has_side_effects=True),
    )(scene_offset, scene_weight, band_gain, heights, scene_ids, u, v)


def solution(mesh):
    placed = (P(("gy", "gz"), "gx"), P(("gy", "gz"), "gx"), P(), P(), P())
    shape = tuple(mesh.shape[name] for name in ("gx", "gy", "gz"))
    return jax.shard_map(
        functools.partial(local, shape), mesh=mesh, in_specs=placed,
        out_specs=P(("gy", "gz"), "gx"), check_vma=False,
    )
```

time: 564 us -> 30.8 us (0.05)
  the two profiles are of different devices: /device:TPU:4 before, /device:TPU:0 now
where the time goes in v1:
time: 30.8 us; the launch traced here: 30.6 us
  Pallas kernels  28.4 us (92%)
  local copies, waits for them, and re-layouts  2.26 us (7%)
    pallas_call x1, Pallas kernels, local(): pl.pallas_call(functools.partial(kernel, sizes), out_shape=jax.ShapeDtype...  28.4 us
    unnamed x1, local copies, waits for them, and re-layouts  2.26 us

profile of v1, /device:TPU:0, one launch (start us, length us, event | category | flops | bytes accessed | tf_op | source)
XLA Modules:
  0.0 30.6 jit_solution(6102149076855702400)
XLA Ops:
  0.0 28.4 %shard_map.73 = f32[512,512]{1,0:T(8,128)} custom-call(f32[16]{0:T(128)} %off_ref.1, f32[16]{0:T(128)} %wgt_ref.1, f32[6]{0:T(128)} %gain_ref.1, f32[512,512]{1,0:T(8,128)} %h_ref.1, s32[512,512]{1,0:T(8,128)} %s_ref.1, f32[16,1,512]{2,1,0:T(1,128)} %constant.4.clone.u_ref, f32[2,1,512]{2,1,0:T(1,128)} %constant.5.clone.v_ref), custom_call_target="tpu_custom_call" | custom-call | tf_op jit(solution)/shard_map/pallas_call | solution.py:411
  28.4 2.3 %copy.9 = f32[512,512]{1,0:T(8,128)} copy(f32[512,512]{1,0:T(8,128)} %shard_map.73) | data formatting | bytes 2097152

commit v2 on v1

--- a/solution.py
+++ b/solution.py
@@ -55,8 +55,8 @@
 
 
 def kernel(
-    sizes, off_ref, wgt_ref, gain_ref, h_ref, s_ref, u_ref, v_ref, out_ref,
-    h_buf, s_buf, u_buf, v_buf, nh, nl, dh, dl, b3, part, slots,
+    sizes, off_ref, wgt_ref, gain_ref, h_ref, s_ref, u_ref, v_ref, z1_ref, q0_ref,
+    q0, h_buf, s_buf, u_buf, v_buf, nh, nl, dh, dl, b3, part, slots,
     own_sem, send0, recv0, send3, recv3, psend, precv,
 ):
     nr, nc, nx, ny, nz, rows_total, cols_total = sizes
@@ -159,6 +159,43 @@
         out = iota(nc, 1) if level == 0 else cols_at(level, 1)
         return band(2 * cols_at(level + 1, 0) - out, 2.0)
 
+    def lookup(masks, table):
+        values = [table[i] for i in range(table.shape[0])]
+        for mask in masks:
+            values = [
+                jnp.where(mask, values[i + 1], values[i]) for i in range(0, len(values), 2)
+            ]
+        return values[0]
+
+    bits = (off_ref.shape[0] - 1).bit_length()
+
+    def level0(rows, cols, valid):
+        ids = s_buf[rows, cols]
+        masks = [(ids & (1 << bit)) != 0 for bit in range(bits)]
+        weight = lookup(masks, wgt_ref)
+        moved = h_buf[rows, cols] + lookup(masks, off_ref)
+        numer = weight * moved
+        if valid is not None:
+            weight = jnp.where(valid, weight, 0.0)
+            numer = jnp.where(valid, numer, 0.0)
+        nh[rows, cols], nl[rows, cols] = split(numer)
+        dh[rows, cols], dl[rows, cols] = split(weight)
+        return moved
+
+    for copy in own:
+        copy.wait()
+
+    step = 32
+
+    def own_rows(i, carry):
+        rows = pl.ds(pl.multiple_of(i * step, step), step)
+        q0[rows, :] = level0(rows, pl.ds(0, nc), None)
+        return carry
+
+    lax.fori_loop(0, nr // step, own_rows, 0)
+
+    reduce0, cols0 = reduce_rows(0), reduce_cols(0)
+
     near = sum(there(*d).astype(jnp.int32) for d in dirs)
     pl.semaphore_wait(barrier, near + (nx + ny + nz - 3))
 
@@ -181,42 +218,6 @@
             for a in range(2):
                 rim(i, a, d).start()
 
-    def lookup(masks, table):
-        values = [table[i] for i in range(table.shape[0])]
-        for mask in masks:
-            values = [
-                jnp.where(mask, values[i + 1], values[i]) for i in range(0, len(values), 2)
-            ]
-        return values[0]
-
-    bits = (off_ref.shape[0] - 1).bit_length()
-
-    def level0(rows, cols, valid):
-        ids = s_buf[rows, cols]
-        masks = [(ids & (1 << bit)) != 0 for bit in range(bits)]
-        weight = lookup(masks, wgt_ref)
-        moved = h_buf[rows, cols] + lookup(masks, off_ref)
-        numer = weight * moved
-        if valid is not None:
-            weight = jnp.where(valid, weight, 0.0)
-            numer = jnp.where(valid, numer, 0.0)
-        nh[rows, cols], nl[rows, cols] = split(numer)
-        dh[rows, cols], dl[rows, cols] = split(weight)
-        return moved
-
-    for copy in own:
-        copy.wait()
-
-    step = 32
-
-    def own_rows(i, carry):
-        rows = pl.ds(pl.multiple_of(i * step, step), step)
-        out_ref[rows, :] = level0(rows, pl.ds(0, nc), None)
-        return carry
-
-    lax.fori_loop(0, nr // step, own_rows, 0)
-
-    reduce0 = reduce_rows(0)
     u_high, u_low = split(u_buf[...])
     pick = iota(16, 0)
     u_rows = jnp.where(
@@ -262,43 +263,44 @@
     for copy in phase(0):
         copy.start()
 
-    for i, d in enumerate(dirs):
-        @pl.when(there(*d))
-        def _():
-            for a in range(2):
-                rim(i, a, d).wait_send()
-
-        @pl.when(there(-d[0], -d[1]))
-        def _():
-            for a in range(2):
-                rim(i, a, d).wait_recv()
+    q0_copy = pltpu.make_async_copy(q0, q0_ref, own_sem.at[4])
+    q0_copy.start()
+
+    def take(ds):
+        for i, d in enumerate(dirs):
+            if d in ds:
+                @pl.when(there(*d))
+                def _():
+                    for a in range(2):
+                        rim(i, a, d).wait_send()
+
+                @pl.when(there(-d[0], -d[1]))
+                def _():
+                    for a in range(2):
+                        rim(i, a, d).wait_recv()
 
     def yes(flag):
         return flag.astype(jnp.int32)
 
     up, down = yes(row > 0), yes(row < blocks - 1)
     west, east = yes(cx > 0), yes(cx < nx - 1)
-
-    def row_ok(p):
-        return jnp.where(p < nr, 1, jnp.where(p < nr + HALO, up, down))
-
-    level0(pl.ds(nr, 2 * HALO), pl.ds(0, nc), jnp.broadcast_to(row_ok(iota(2 * HALO, 0) + nr), (2 * HALO, nc)) > 0)
     side_ok = jnp.where(iota(2 * SIDE, 1) < SIDE, west, east)
+    rim_ok = jnp.where(iota(2 * HALO, 0) < HALO, up, down)
+    body, rim_r = pl.ds(0, nr), pl.ds(nr, 2 * HALO)
+    middle, side_c = pl.ds(0, nc), pl.ds(nc, 2 * SIDE)
+
+    take([d for d in dirs if d[0] == 0])
 
     def side_rows(i, carry):
         rows = pl.ds(pl.multiple_of(i * step, step), step)
-        level0(rows, pl.ds(nc, 2 * SIDE), (row_ok(iota(step, 0) + i * step) * side_ok) > 0)
+        level0(rows, side_c, jnp.broadcast_to(side_ok, (step, 2 * SIDE)) > 0)
         return carry
 
-    lax.fori_loop(0, (nr + 2 * HALO) // step, side_rows, 0)
-
-    rim_r, side_c = pl.ds(nr, 2 * HALO), pl.ds(nc, 2 * SIDE)
-    cols0 = reduce_cols(0)
+    lax.fori_loop(0, nr // step, side_rows, 0)
 
     def level1(t_own, high, low):
-        t_own = t_own[:r1, :] + dot(rim0, high[rim_r, pl.ds(0, nc)]) + dot(rim0, low[rim_r, pl.ds(0, nc)])
-        t_side = dot(reduce0, high[:, side_c]) + dot(reduce0, low[:, side_c])
-        return right(t_own, cols0[:nc]) + right(t_side, cols0[nc:])
+        t_side = dot(reduce0[:, :nr], high[body, side_c]) + dot(reduce0[:, :nr], low[body, side_c])
+        return right(t_own[:r1, :], cols0[:nc]) + right(t_side, cols0[nc:])
 
     n1, d1 = level1(tn, nh, nl), level1(td, dh, dl)
 
@@ -314,8 +316,41 @@
     pick_n = band(jnp.where(own_out < w3, in2 - 2 * own_out, FAR), 1.0)
     pick_d = band(jnp.where(own_out < w3, FAR, in2 - 2 * (own_out - w3)), 1.0)
     own_rows3 = band(rows_at(2, 1) - 2 * iota(t3, 0), 1.0)
-    both = right(n2, pick_n) + right(d2, pick_d)
-    b3[1, pl.ds(EDGE3, t3), :] = left(own_rows3, both)
+    both = left(own_rows3, right(n2, pick_n) + right(d2, pick_d))
+
+    def ends(count):
+        p = iota(32, 0)
+        return jnp.where(p < 16, p, count - 32 + p)
+
+    def ends_in(count):
+        p = iota(32, 1)
+        return jnp.where(p < 16, p, count - 32 + p)
+
+    ends0 = band(
+        (iota(2 * HALO, 1) + jnp.where(iota(2 * HALO, 1) < HALO, -HALO, nr - HALO))
+        - 2 * fold(ends(r1) - 8, row0, rows_total, 1), 1.0,
+    )
+    ends1 = band((ends_in(r1) - 8) - 2 * fold(ends(r2) - 8, row0, rows_total, 2), 1.0)
+    ends2 = band((ends_in(r2) - 8) - 2 * ends(t3), 1.0)
+
+    def patch(x, e):
+        n = x.shape[0]
+        return jnp.concatenate([x[:16] + e[:16], x[16 : n - 16], x[n - 16 :] + e[16:]], axis=0)
+
+    take([d for d in dirs if d[0] != 0])
+    level0(rim_r, middle, jnp.broadcast_to(rim_ok, (2 * HALO, nc)) > 0)
+    level0(rim_r, side_c, jnp.broadcast_to(rim_ok * side_ok, (2 * HALO, 2 * SIDE)) > 0)
+
+    def pair(x):
+        return x[:32], x[32:]
+
+    stacked = dot(jnp.concatenate([nh[rim_r, :], dh[rim_r, :]], axis=0), cols0) + dot(
+        jnp.concatenate([nl[rim_r, :], dl[rim_r, :]], axis=0), cols0
+    )
+    e1 = [left(ends0, x) for x in pair(stacked)]
+    e2 = [left(ends1, x) for x in pair(right(jnp.concatenate(e1, axis=0), cols1))]
+    e3 = left(ends2, right(e2[0], pick_n) + right(e2[1], pick_d))
+    b3[1, pl.ds(EDGE3, t3), :] = patch(both, e3)
 
     def rim3(i, d):
         drow, dcol = d
@@ -337,6 +372,7 @@
         def _():
             rim3(i, d).start()
 
+    n1, d1, n2, d2 = patch(n1, e1[0]), patch(d1, e1[1]), patch(n2, e2[0]), patch(d2, e2[1])
     q1 = jnp.where(d1 > 0, n1 / d1, 0.0)
     q2 = jnp.where(d2 > 0, n2 / d2, 0.0)
     part[2] = finish(1)
@@ -345,8 +381,8 @@
 
     rows_ = [None, None, None] + [reduce_rows(level) for level in (3, 4, 5)]
     cols_ = [None, None, None] + [reduce_cols(level) for level in (3, 4, 5)]
-    up_rows = [expand_rows(level) for level in range(6)]
-    up_cols = [expand_cols(level) for level in range(6)]
+    up_rows = [None] + [expand_rows(level) for level in range(1, 6)]
+    up_cols = [None] + [expand_cols(level) for level in range(1, 6)]
 
     for i, d in enumerate(dirs):
         @pl.when(there(*d))
@@ -393,8 +429,35 @@
     for level, q, ok in levels:
         grown = left(up_rows[level], right(z, up_cols[level]))
         z = jnp.where(ok, grown + (gain_ref[level] - gain_ref[level - 1]) * q, 0.0)
-    wide = right(z, up_cols[0])
-    out_ref[...] = gain_ref[0] * out_ref[...] + left(up_rows[0], wide)
+    z1_ref[...] = z
+    q0_copy.wait()
+
+
+def last(gain_ref, z_ref, q_hbm, out_ref, q_buf, sem):
+    nr, nc = out_ref.shape
+    block = nr // 4
+    copies = [
+        pltpu.make_async_copy(
+            q_hbm.at[pl.ds(i * block, block), :], q_buf.at[pl.ds(i * block, block), :], sem.at[i]
+        )
+        for i in range(4)
+    ]
+    for copy in copies:
+        copy.start()
+    tall = block // 2 + 16
+
+    def iota(n, dim):
+        return lax.broadcasted_iota(jnp.int32, (n, 1) if dim == 0 else (1, n), dim)
+
+    cols = band(2 * (iota(z_ref.shape[1], 0) - 8) - iota(nc, 1), 2.0)
+    rows = band(2 * (iota(tall, 1) - 8) - iota(block, 0), 2.0)
+    gain = gain_ref[0]
+    wide = right(z_ref[...], cols)
+    for i in range(4):
+        grown = left(rows, wide[i * block // 2 : i * block // 2 + tall])
+        copies[i].wait()
+        here = pl.ds(i * block, block)
+        out_ref[here, :] = gain * q_buf[here, :] + grown
 
 
 def local(mesh_shape, heights, scene_ids, scene_offset, scene_weight, band_gain):
@@ -408,12 +471,16 @@
     peers = nx + ny + nz - 3
     smem = pl.BlockSpec(memory_space=pltpu.SMEM)
     hbm = pl.BlockSpec(memory_space=pl.ANY)
-    return pl.pallas_call(
+    z1, q0 = pl.pallas_call(
         functools.partial(kernel, sizes),
-        out_shape=jax.ShapeDtypeStruct((nr, nc), F32),
+        out_shape=(
+            jax.ShapeDtypeStruct((nr // 2 + 16, nc // 2 + 128), F32),
+            jax.ShapeDtypeStruct((nr, nc), F32),
+        ),
         in_specs=[smem, smem, smem, hbm, hbm, hbm, hbm],
-        out_specs=pl.BlockSpec(memory_space=pltpu.VMEM),
+        out_specs=(pl.BlockSpec(memory_space=pltpu.VMEM), hbm),
         scratch_shapes=[
+            pltpu.VMEM((nr, nc), F32),
             pltpu.VMEM(ext, F32),
             pltpu.VMEM(ext, jnp.int32),
             pltpu.VMEM((1, nr), F32),
@@ -425,7 +492,7 @@
             pltpu.VMEM((3, nr // 8 + 2 * EDGE3, nc // 4), F32),
             pltpu.VMEM((3, 8, 128), F32),
             pltpu.VMEM((peers, 8, 128), F32),
-            pltpu.SemaphoreType.DMA((4,)),
+            pltpu.SemaphoreType.DMA((5,)),
             pltpu.SemaphoreType.DMA((16,)),
             pltpu.SemaphoreType.DMA((16,)),
             pltpu.SemaphoreType.DMA((8,)),
@@ -435,6 +502,14 @@
         ],
         compiler_params=pltpu.CompilerParams(collective_id=0, has_side_effects=True),
     )(scene_offset, scene_weight, band_gain, heights, scene_ids, u, v)
+    vmem = pl.BlockSpec(memory_space=pltpu.VMEM)
+    return pl.pallas_call(
+        last,
+        out_shape=jax.ShapeDtypeStruct((nr, nc), F32),
+        in_specs=[smem, vmem, hbm],
+        out_specs=vmem,
+        scratch_shapes=[pltpu.VMEM((nr, nc), F32), pltpu.SemaphoreType.DMA((4,))],
+    )(band_gain, z1, q0)
 
 
 def solution(mesh):

time: 30.8 us -> 28.6 us (0.929)
  local copies, waits for them, and re-layouts: 2.26 us -> 0 us
    unnamed x1 -> x0, local copies, waits for them, and re-layouts: 2.26 us -> none
    pallas_call x1 -> x2, Pallas kernels: 28.4 us -> 28.4 us  [the longest x1 24.8 us: local(): pl.pallas_call(functools.partial(kernel, sizes), out_shape=(jax.ShapeDtyp...]
where the time goes in v2:
time: 28.6 us; the launch traced here: 28.4 us
  Pallas kernels  28.4 us (99%)
    pallas_call x1, Pallas kernels, local(): pl.pallas_call(functools.partial(kernel, sizes), out_shape=(jax.ShapeDtyp...  24.8 us
    pallas_call x1, Pallas kernels, local(): pl.pallas_call(last, out_shape=jax.ShapeDtypeStruct((nr, nc), F32), in_sp...  3.63 us

profile of v2, /device:TPU:0, one launch (start us, length us, event | category | flops | bytes accessed | tf_op | source)
XLA Modules:
  0.0 28.4 jit_solution(16778045027306137416)
XLA Ops:
  0.0 24.8 %shard_map.73 = (f32[272,384]{1,0:T(8,128)}, f32[512,512]{1,0:T(8,128)}) custom-call(f32[16]{0:T(128)} %off_ref.1, f32[16]{0:T(128)} %wgt_ref.1, f32[6]{0:T(128)} %gain_ref.3, f32[512,512]{1,0:T(8,128)} %h_ref.1, s32[512,512]{1,0:T(8,128)} %s_ref.1, f32[16,1,512]{2,1,0:T(1,128)} %constant.4.clone.u_ref, f32[2,1,512]{2,1,0:T(1,128)} %constant.5.clone.v_ref), custom_call_target="tpu_custom_call" | custom-call | tf_op jit(solution)/shard_map/pallas_call | solution.py:474
  24.8 3.6 %shard_map.74 = f32[512,512]{1,0:T(8,128)} custom-call(f32[6]{0:T(128)} %gain_ref.3, f32[272,384]{1,0:T(8,128)} %get-tuple-element.7.z_ref, f32[512,512]{1,0:T(8,128)} %get-tuple-element.8.q_hbm), custom_call_target="tpu_custom_call" | custom-call | tf_op jit(solution)/shard_map/pallas_call | solution.py:506

commit v3 on v2

--- a/solution.py
+++ b/solution.py
@@ -194,8 +194,6 @@
 
     lax.fori_loop(0, nr // step, own_rows, 0)
 
-    reduce0, cols0 = reduce_rows(0), reduce_cols(0)
-
     near = sum(there(*d).astype(jnp.int32) for d in dirs)
     pl.semaphore_wait(barrier, near + (nx + ny + nz - 3))
 
@@ -218,22 +216,32 @@
             for a in range(2):
                 rim(i, a, d).start()
 
+    def dot(a, b):
+        return jnp.dot(a, b, preferred_element_type=F32)
+
+    own_out = iota(2 * w3, 1)
+    in2 = cols_at(2, 0)
+    pick_n = band(jnp.where(own_out < w3, in2 - 2 * own_out, FAR), 1.0)
+    pick_d = band(jnp.where(own_out < w3, FAR, in2 - 2 * (own_out - w3)), 1.0)
+    own_rows3 = band(rows_at(2, 1) - 2 * iota(t3, 0), 1.0)
+    reduce0, rows1 = reduce_rows(0), reduce_rows(1)
+    rows03 = dot(dot(own_rows3, rows1).astype(BF16), reduce0)
+    rows03 = jnp.concatenate(split(rows03), axis=0)
     u_high, u_low = split(u_buf[...])
     pick = iota(16, 0)
     u_rows = jnp.where(
         pick == 0, u_high.astype(F32), jnp.where(pick == 1, u_low.astype(F32), 0.0)
     ).astype(BF16)
-    top = jnp.concatenate([reduce0[:, :nr], u_rows], axis=0)
-    rim0 = reduce0[:, nr:]
-
-    def dot(a, b):
-        return jnp.dot(a, b, preferred_element_type=F32)
-
-    tn = dot(top, nh[pl.ds(0, nr), pl.ds(0, nc)]) + dot(top, nl[pl.ds(0, nr), pl.ds(0, nc)])
-    td = dot(top, dh[pl.ds(0, nr), pl.ds(0, nc)]) + dot(top, dl[pl.ds(0, nr), pl.ds(0, nc)])
+    top = jnp.concatenate([rows03[:, :nr], u_rows], axis=0)
+
+    def own_part(high, low):
+        rows, cols = pl.ds(0, nr), pl.ds(0, nc)
+        return dot(top, high[rows, cols]) + dot(top, low[rows, cols])
+
+    tn, td = own_part(nh, nl), own_part(dh, dl)
     v_row = v_buf[...]
-    sum_n = jnp.sum(tn[r1:, :] * v_row)
-    sum_d = jnp.sum(td[r1:, :] * v_row)
+    sum_n = jnp.sum(tn[2 * t3 :, :] * v_row)
+    sum_d = jnp.sum(td[2 * t3 :, :] * v_row)
 
     tile_row = lax.broadcasted_iota(jnp.int32, (8, 128), 0)
     part[0] = jnp.where(tile_row == 0, sum_n, jnp.where(tile_row == 1, sum_d, 0.0))
@@ -298,59 +306,57 @@
 
     lax.fori_loop(0, nr // step, side_rows, 0)
 
-    def level1(t_own, high, low):
-        t_side = dot(reduce0[:, :nr], high[body, side_c]) + dot(reduce0[:, :nr], low[body, side_c])
-        return right(t_own[:r1, :], cols0[:nc]) + right(t_side, cols0[nc:])
-
-    n1, d1 = level1(tn, nh, nl), level1(td, dh, dl)
+    cols0, cols1 = reduce_cols(0), reduce_cols(1)
+    cols02 = dot(cols0, cols1).astype(BF16)
+    cols03 = [split(dot(cols02, pick)) for pick in (pick_n, pick_d)]
+
+    def side_part(t, high, low):
+        t_side = dot(rows03[:, :nr], high[body, side_c]) + dot(rows03[:, :nr], low[body, side_c])
+        t = jnp.concatenate([t[: 2 * t3], t_side], axis=1)
+        return t[:t3] + t[t3:]
+
+    tn, td = side_part(tn, nh, nl), side_part(td, dh, dl)
 
     part[1] = finish(0)
     for copy in phase(1):
         copy.start()
 
-    rows1, cols1 = reduce_rows(1), reduce_cols(1)
-    n2, d2 = left(rows1, right(n1, cols1)), left(rows1, right(d1, cols1))
-
-    own_out = iota(2 * w3, 1)
-    in2 = cols_at(2, 0)
-    pick_n = band(jnp.where(own_out < w3, in2 - 2 * own_out, FAR), 1.0)
-    pick_d = band(jnp.where(own_out < w3, FAR, in2 - 2 * (own_out - w3)), 1.0)
-    own_rows3 = band(rows_at(2, 1) - 2 * iota(t3, 0), 1.0)
-    both = left(own_rows3, right(n2, pick_n) + right(d2, pick_d))
-
-    def ends(count):
-        p = iota(32, 0)
-        return jnp.where(p < 16, p, count - 32 + p)
-
-    def ends_in(count):
-        p = iota(32, 1)
-        return jnp.where(p < 16, p, count - 32 + p)
-
-    ends0 = band(
-        (iota(2 * HALO, 1) + jnp.where(iota(2 * HALO, 1) < HALO, -HALO, nr - HALO))
-        - 2 * fold(ends(r1) - 8, row0, rows_total, 1), 1.0,
+    half, start = nr // 4, nr // 2 - 32
+    reduce0_b = band(
+        start + iota(nr - start, 1) - 2 * fold(iota(r1 - half, 0) + (half - 8), row0, rows_total, 1), 1.0
     )
-    ends1 = band((ends_in(r1) - 8) - 2 * fold(ends(r2) - 8, row0, rows_total, 2), 1.0)
-    ends2 = band((ends_in(r2) - 8) - 2 * ends(t3), 1.0)
-
-    def patch(x, e):
-        n = x.shape[0]
-        return jnp.concatenate([x[:16] + e[:16], x[16 : n - 16], x[n - 16 :] + e[16:]], axis=0)
+
+    def level1(x):
+        t = [dot(reduce0[:half, : nr // 2], part_[pl.ds(0, nr // 2), :]) for part_ in x]
+        b = [dot(reduce0_b, part_[pl.ds(start, nr - start), :]) for part_ in x]
+        t = jnp.concatenate([t[0] + t[1], b[0] + b[1]], axis=0)
+        low, high = split(t)
+
+        def wide(k0, k1, n0, n1):
+            return dot(low[:, k0:k1], cols0[k0:k1, n0:n1]) + dot(high[:, k0:k1], cols0[k0:k1, n0:n1])
+
+        edge = nc // 2
+        return jnp.concatenate(
+            [
+                wide(0, nc + SIDE, 0, edge),
+                wide(nc - SIDE, nc, edge, c1) + wide(nc + SIDE, nc + 2 * SIDE, edge, c1),
+            ],
+            axis=1,
+        )
+
+    n1, d1 = level1((nh, nl)), level1((dh, dl))
 
     take([d for d in dirs if d[0] != 0])
     level0(rim_r, middle, jnp.broadcast_to(rim_ok, (2 * HALO, nc)) > 0)
     level0(rim_r, side_c, jnp.broadcast_to(rim_ok * side_ok, (2 * HALO, 2 * SIDE)) > 0)
 
-    def pair(x):
-        return x[:32], x[32:]
-
-    stacked = dot(jnp.concatenate([nh[rim_r, :], dh[rim_r, :]], axis=0), cols0) + dot(
-        jnp.concatenate([nl[rim_r, :], dl[rim_r, :]], axis=0), cols0
-    )
-    e1 = [left(ends0, x) for x in pair(stacked)]
-    e2 = [left(ends1, x) for x in pair(right(jnp.concatenate(e1, axis=0), cols1))]
-    e3 = left(ends2, right(e2[0], pick_n) + right(e2[1], pick_d))
-    b3[1, pl.ds(EDGE3, t3), :] = patch(both, e3)
+    def rim_part(t, high, low, cols):
+        e = dot(rows03[:, nr:], high[rim_r, :]) + dot(rows03[:, nr:], low[rim_r, :])
+        t = t + e[:t3] + e[t3:]
+        t_high, t_low = split(t)
+        return dot(t_high, cols[0]) + dot(t_low, cols[0]) + dot(t_high, cols[1])
+
+    b3[1, pl.ds(EDGE3, t3), :] = rim_part(tn, nh, nl, cols03[0]) + rim_part(td, dh, dl, cols03[1])
 
     def rim3(i, d):
         drow, dcol = d
@@ -372,12 +378,26 @@
         def _():
             rim3(i, d).start()
 
-    n1, d1, n2, d2 = patch(n1, e1[0]), patch(d1, e1[1]), patch(n2, e2[0]), patch(d2, e2[1])
-    q1 = jnp.where(d1 > 0, n1 / d1, 0.0)
-    q2 = jnp.where(d2 > 0, n2 / d2, 0.0)
+    def ends(count):
+        p = iota(32, 0)
+        return jnp.where(p < 16, p, count - 32 + p)
+
+    rim_in = iota(2 * HALO, 1)
+    rim_in = rim_in + jnp.where(rim_in < HALO, -HALO, nr - HALO)
+    ends0 = band(rim_in - 2 * fold(ends(r1) - 8, row0, rows_total, 1), 1.0)
+
+    def patch(x, high, low):
+        e = left(ends0, dot(high[rim_r, :], cols0) + dot(low[rim_r, :], cols0))
+        n = x.shape[0]
+        return jnp.concatenate([x[:16] + e[:16], x[16 : n - 16], x[n - 16 :] + e[16:]], axis=0)
+
+    n1, d1 = patch(n1, nh, nl), patch(d1, dh, dl)
     part[2] = finish(1)
     for copy in phase(2):
         copy.start()
+    q1 = jnp.where(d1 > 0, n1 / d1, 0.0)
+    n2, d2 = left(rows1, right(n1, cols1)), left(rows1, right(d1, cols1))
+    q2 = jnp.where(d2 > 0, n2 / d2, 0.0)
 
     rows_ = [None, None, None] + [reduce_rows(level) for level in (3, 4, 5)]
     cols_ = [None, None, None] + [reduce_cols(level) for level in (3, 4, 5)]
@@ -433,8 +453,8 @@
     q0_copy.wait()
 
 
-def last(gain_ref, z_ref, q_hbm, out_ref, q_buf, sem):
-    nr, nc = out_ref.shape
+def last(gain_ref, z_ref, q_hbm, out_ref, q_buf, out_buf, sem):
+    nr, nc = out_buf.shape
     block = nr // 4
     copies = [
         pltpu.make_async_copy(
@@ -453,11 +473,16 @@
     rows = band(2 * (iota(tall, 1) - 8) - iota(block, 0), 2.0)
     gain = gain_ref[0]
     wide = right(z_ref[...], cols)
+    writes = []
     for i in range(4):
         grown = left(rows, wide[i * block // 2 : i * block // 2 + tall])
         copies[i].wait()
         here = pl.ds(i * block, block)
-        out_ref[here, :] = gain * q_buf[here, :] + grown
+        out_buf[here, :] = gain * q_buf[here, :] + grown
+        writes.append(pltpu.make_async_copy(out_buf.at[here, :], out_ref.at[here, :], sem.at[4 + i]))
+        writes[-1].start()
+    for write in writes:
+        write.wait()
 
 
 def local(mesh_shape, heights, scene_ids, scene_offset, scene_weight, band_gain):
@@ -507,8 +532,12 @@
         last,
         out_shape=jax.ShapeDtypeStruct((nr, nc), F32),
         in_specs=[smem, vmem, hbm],
-        out_specs=vmem,
-        scratch_shapes=[pltpu.VMEM((nr, nc), F32), pltpu.SemaphoreType.DMA((4,))],
+        out_specs=hbm,
+        scratch_shapes=[
+            pltpu.VMEM((nr, nc), F32),
+            pltpu.VMEM((nr, nc), F32),
+            pltpu.SemaphoreType.DMA((8,)),
+        ],
     )(band_gain, z1, q0)
 
 

time: 28.6 us -> 27.1 us (0.948)
  Pallas kernels: 28.4 us -> 26.9 us
    pallas_call x1, Pallas kernels: 24.8 us -> 23.4 us  [local(): pl.pallas_call(functools.partial(kernel, sizes), out_shape=(jax.ShapeDtyp...]
where the time goes in v3:
time: 27.1 us; the launch traced here: 26.9 us
  Pallas kernels  26.9 us (99%)
    pallas_call x1, Pallas kernels, local(): pl.pallas_call(functools.partial(kernel, sizes), out_shape=(jax.ShapeDtyp...  23.4 us
    pallas_call x1, Pallas kernels, local(): pl.pallas_call(last, out_shape=jax.ShapeDtypeStruct((nr, nc), F32), in_sp...  3.41 us

profile of v3, /device:TPU:0, one launch (start us, length us, event | category | flops | bytes accessed | tf_op | source)
XLA Modules:
  0.0 26.9 jit_solution(10998826809693551660)
XLA Ops:
  0.0 23.4 %shard_map.73 = (f32[272,384]{1,0:T(8,128)}, f32[512,512]{1,0:T(8,128)}) custom-call(f32[16]{0:T(128)} %off_ref.1, f32[16]{0:T(128)} %wgt_ref.1, f32[6]{0:T(128)} %gain_ref.3, f32[512,512]{1,0:T(8,128)} %h_ref.1, s32[512,512]{1,0:T(8,128)} %s_ref.1, f32[16,1,512]{2,1,0:T(1,128)} %constant.4.clone.u_ref, f32[2,1,512]{2,1,0:T(1,128)} %constant.5.clone.v_ref), custom_call_target="tpu_custom_call" | custom-call | tf_op jit(solution)/shard_map/pallas_call | solution.py:499
  23.5 3.4 %shard_map.74 = f32[512,512]{1,0:T(8,128)} custom-call(f32[6]{0:T(128)} %gain_ref.3, f32[272,384]{1,0:T(8,128)} %get-tuple-element.7.z_ref, f32[512,512]{1,0:T(8,128)} %get-tuple-element.8.q_hbm), custom_call_target="tpu_custom_call" | custom-call | tf_op jit(solution)/shard_map/pallas_call | solution.py:531
